TPU v7x, 256 devices: a whole 4x4x8 slice. The times are simulated.
256 devices in a mesh: row: 16 (over z, core), col: 16 (over y, x).
Axes of the slice: x: 4, y: 4, z: 8, core: 2. Of those that a mesh axis runs over, the one named last changes fastest.
Arguments:
- rhs: float32 [24576, 12288], P('row', 'col'), may hold values from -6 to 6
- panels_l: float32 [4, 24576, 512], P(None, 'row', 'col'), may hold values from -0.25 to 0.25
- diag_inverse: float32 [4, 512, 512], P(None, None, 'col'), may hold values from -1.5 to 1.5, as said below
Outputs:
- solved_rhs: float32 [24576, 12288], P('row', 'col')
Inputs may be any that keep to these rules, and one draw needn't show every extreme that they name: `diag_inverse`: each tile is lower triangular with diagonal entries between 0.5 and 1.5.
All inputs are finite; a program needn't handle non-finite values.
Results may differ from a plain program's by a relative error of at most 0.00016.
Values sent between devices are 32-bit elements; how exact they have to be, the bound alone decides.
A program may use at most 128 MiB of HBM per device.

v0:
```python
import jax
import jax.numpy as jnp
from jax import lax
from jax.sharding import PartitionSpec as P


def spread(x, axis, root):
    mine = lax.axis_index(axis) == root
    return lax.psum(jnp.where(mine, x, jnp.zeros_like(x)), axis)


def exact_dot(left, right):
    return jnp.dot(left, right, precision=lax.Precision.HIGHEST, preferred_element_type=jnp.float32)


def per_device(rhs, panels_l, diag_inverse):
    rows_here = rhs.shape[0]
    width = diag_inverse.shape[1]
    count = panels_l.shape[0]
    my_row = lax.axis_index("row")
    global_rows = my_row * rows_here + lax.iota(jnp.int32, rows_here)
    work = rhs
    for k in range(count):
        factor_cols = lax.all_gather(panels_l[k], "col", axis=1, tiled=True)
        inverse_tile = lax.all_gather(diag_inverse[k], "col", axis=1, tiled=True)
        owner = k * width // rows_here
        offset = k * width - owner * rows_here
        strip = work[offset : offset + width]
        is_owner = my_row == owner
        solved_here = lax.cond(
            is_owner,
            lambda: exact_dot(inverse_tile, strip),
            lambda: jnp.zeros(strip.shape, jnp.float32),
        )
        solved = spread(solved_here, "row", owner)
        update = exact_dot(factor_cols, solved)
        below = (global_rows >= (k + 1) * width)[:, None]
        work = jnp.where(below, work - update, work)
        work = work.at[offset : offset + width].set(
            jnp.where(is_owner, solved, work[offset : offset + width])
        )
    return work


def solution(mesh):
    in_specs = (P("row", "col"), P(None, "row", "col"), P(None, None, "col"))
    out_specs = P("row", "col")
    return jax.shard_map(
        per_device, mesh=mesh, in_specs=in_specs, out_specs=out_specs, check_vma=False
    )
```

profile of v0, /device:TPU:1, one launch (start us, length us, event | category | flops | bytes accessed | tf_op | source)
XLA Modules:
  0.0 919.6 jit_solution(2855108133627082533)
XLA Ops:
  6.5 1.0 fusion.27
  7.5 0.7 copy.52
  8.3 51.0 %all-gather.17.cloned.1.call-done = f32[1,512,512]{1,0,2:T(1,128)} async-done(((f32[1,512,32]{1,0,2:T(1,128)}), f32[1,512,512]{1,0,2:T(1,128)}) %all-gather.17.cloned.1.call-update) | async-done | bytes 1048592 | tf_op jit(solution)/shard_map/all_gather | solution.py:25
  59.3 1.3 copy.69
  60.6 0.2 conditional.4
  60.6 0.2 broadcast.87.clone
  60.8 1.4 broadcast_select_fusion.3
  62.2 1.1 copy-done.7
  63.3 0.9 fusion.26
  64.2 0.0 all-gather.21.cloned.1.call-start
  64.3 0.7 copy.53
  65.0 0.5 all-gather.23.cloned.1.call-update
  65.6 6.0 copy.21
  71.7 105.5 %all-reduce.5.cloned.1.call-done = f32[512,768]{0,1:T(8,128)} async-done(((f32[512,768]{0,1:T(8,128)}), f32[512,768]{0,1:T(8,128)}) %all-reduce.5.cloned.1.call-update) | async-done | bytes 1572880 | tf_op jit(solution)/shard_map/psum | solution.py:9
  177.2 55.1 %all-gather.19.cloned.1.call-done = f32[1,1536,512]{1,2,0:T(8,128)} async-done(((f32[1,1536,32]{1,2,0:T(8,128)}), f32[1,1536,512]{1,2,0:T(8,128)}) %all-gather.19.cloned.1.call-update) | async-done | bytes 3145744 | tf_op jit(solution)/shard_map/all_gather | solution.py:24
  232.3 12.0 %subtract_select_fusion.3 = f32[1536,768]{0,1:T(8,128)} fusion(f32[1536,768]{0,1:T(8,128)} %copy.21, f32[512,768]{0,1:T(8,128)} %all-reduce.5.cloned.1.call-done, f32[1,1536,512]{1,2,0:T(8,128)} %all-gather.19.cloned.1.call-done, pred[1536]{0:T(1024)(128)(4,1)S(1)} %fusion.22), kind=kOutput, calls=%fused_computation.17 | convolution fusion | flops 7250116608 | bytes 14157312 | tf_op jit(solution)/shard_map/dot_general | solution.py:13
  244.3 2.9 fusion.21
  247.2 32.6 %all-gather.21.cloned.1.call-done = f32[1,512,512]{1,0,2:T(1,128)} async-done(((f32[1,512,32]{1,0,2:T(1,128)}), f32[1,512,512]{1,0,2:T(1,128)}) %all-gather.21.cloned.1.call-update) | async-done | bytes 1048592 | tf_op jit(solution)/shard_map/all_gather | solution.py:25
  279.8 0.4 conditional.5
  279.8 0.2 broadcast.88.clone
  280.2 1.3 broadcast_select_fusion.2
  281.6 0.7 copy.54
  282.3 0.7 all-gather.27.cloned.1.call-update
  283.1 52.3 %all-gather.23.cloned.1.call-done = f32[1,1536,512]{1,2,0:T(8,128)} async-done(((f32[1,1536,32]{1,2,0:T(8,128)}), f32[1,1536,512]{1,2,0:T(8,128)}) %all-gather.23.cloned.1.call-update) | async-done | bytes 3145744 | tf_op jit(solution)/shard_map/all_gather | solution.py:24
  335.5 115.4 %all-reduce.7.cloned.1.call-done = f32[512,768]{0,1:T(8,128)} async-done(((f32[512,768]{0,1:T(8,128)}), f32[512,768]{0,1:T(8,128)}) %all-reduce.7.cloned.1.call-update) | async-done | bytes 1572880 | tf_op jit(solution)/shard_map/psum | solution.py:9
  450.9 12.9 %subtract_select_fusion.2 = f32[1536,768]{0,1:T(8,128)} fusion(f32[1536,768]{0,1:T(8,128)} %fusion.21, f32[512,768]{0,1:T(8,128)} %all-reduce.7.cloned.1.call-done, f32[1,1536,512]{1,2,0:T(8,128)} %all-gather.23.cloned.1.call-done, pred[1536]{0:T(1024)(128)(4,1)S(1)} %fusion.23), kind=kOutput, calls=%fused_computation.16 | convolution fusion | flops 7250116608 | bytes 14157312 | tf_op jit(solution)/shard_map/dot_general | solution.py:13
  463.8 2.9 fusion.20
  466.7 32.8 %all-gather.25.cloned.1.call-done = f32[1,512,512]{1,0,2:T(1,128)} async-done(((f32[1,512,32]{1,0,2:T(1,128)}), f32[1,512,512]{1,0,2:T(1,128)}) %all-gather.25.cloned.1.call-update) | async-done | bytes 1048592 | tf_op jit(solution)/shard_map/all_gather | solution.py:25
  499.5 0.2 conditional.6
  499.5 0.2 broadcast.89.clone
  499.7 1.3 broadcast_select_fusion.1
  501.1 0.7 copy.55
  501.9 0.7 all-gather.31.cloned.1.call-update
  502.6 0.3 all-reduce.11.cloned.1.call-start
  502.8 52.5 %all-gather.27.cloned.1.call-done = f32[1,1536,512]{1,2,0:T(8,128)} async-done(((f32[1,1536,32]{1,2,0:T(8,128)}), f32[1,1536,512]{1,2,0:T(8,128)}) %all-gather.27.cloned.1.call-update) | async-done | bytes 3145744 | tf_op jit(solution)/shard_map/all_gather | solution.py:24
  555.3 115.6 %all-reduce.9.cloned.1.call-done = f32[512,768]{0,1:T(8,128)} async-done(((f32[512,768]{0,1:T(8,128)}), f32[512,768]{0,1:T(8,128)}) %all-reduce.9.cloned.1.call-update) | async-done | bytes 1572880 | tf_op jit(solution)/shard_map/psum | solution.py:9
  670.9 12.9 %subtract_select_fusion.1 = f32[1536,768]{0,1:T(8,128)} fusion(f32[1536,768]{0,1:T(8,128)} %fusion.20, f32[512,768]{0,1:T(8,128)} %all-reduce.9.cloned.1.call-done, f32[1,1536,512]{1,2,0:T(8,128)} %all-gather.27.cloned.1.call-done, pred[1536]{0:T(1024)(128)(4,1)S(1)} %fusion.24), kind=kOutput, calls=%fused_computation.15 | convolution fusion | flops 7250116608 | bytes 14157312 | tf_op jit(solution)/shard_map/dot_general | solution.py:13
  683.8 2.9 fusion.19
  686.7 32.7 %all-gather.29.cloned.1.call-done = f32[1,512,512]{1,0,2:T(1,128)} async-done(((f32[1,512,32]{1,0,2:T(1,128)}), f32[1,512,512]{1,0,2:T(1,128)}) %all-gather.29.cloned.1.call-update) | async-done | bytes 1048592 | tf_op jit(solution)/shard_map/all_gather | solution.py:25
  719.4 10.5 %conditional.7 = (f32[512,768]{0,1:T(8,128)S(1)}) conditional(s32[]{:T(128)} %convert_element_type.9, () %tuple.51, (f32[1536,768]{0,1:T(8,128)}, f32[1,512,512]{1,0,2:T(1,128)}) %tuple.52), branch_computations={%region_9.10_spmd, %region_10.11_spmd} | conditional | flops 2415919104 | bytes 17825828 | solution.py:30
  719.4 6.1 copy.32
  725.5 4.1 fusion.10
  729.8 1.3 broadcast_select_fusion
  731.2 44.0 %all-gather.31.cloned.1.call-done = f32[1,1536,512]{1,2,0:T(8,128)} async-done(((f32[1,1536,32]{1,2,0:T(8,128)}), f32[1,1536,512]{1,2,0:T(8,128)}) %all-gather.31.cloned.1.call-update) | async-done | bytes 3145744 | tf_op jit(solution)/shard_map/all_gather | solution.py:24
  775.2 115.4 %all-reduce.11.cloned.1.call-done = f32[512,768]{0,1:T(8,128)} async-done(((f32[512,768]{0,1:T(8,128)}), f32[512,768]{0,1:T(8,128)}) %all-reduce.11.cloned.1.call-update) | async-done | bytes 1572880 | tf_op jit(solution)/shard_map/psum | solution.py:9
  890.6 13.1 %subtract_select_fusion = f32[1536,768]{0,1:T(8,128)} fusion(f32[1536,768]{0,1:T(8,128)} %fusion.19, f32[512,768]{0,1:T(8,128)} %all-reduce.11.cloned.1.call-done, f32[1,1536,512]{1,2,0:T(8,128)} %all-gather.31.cloned.1.call-done, pred[1536]{0:T(1024)(128)(4,1)S(1)} %fusion.25), kind=kOutput, calls=%fused_computation.14 | convolution fusion | flops 7250116608 | bytes 14157312 | tf_op jit(solution)/shard_map/dot_general | solution.py:13
  903.6 3.0 fusion.18
  906.7 6.0 copy.35
  (34 shorter events, 0.6 us)
Async XLA Ops:
  6.5 52.8 %all-gather.17.cloned.1.call-start = ((), (), s32[]{:S(2)}) async-start(), calls=%async_computation.4 | async-start | bytes 1114112 | tf_op jit(solution)/shard_map/all_gather | solution.py:25
  8.2 169.0 %all-reduce.5.cloned.1.call-start = ((), (), s32[]{:S(2)}) async-start(), calls=%async_computation | async-start | bytes 3145728 | tf_op jit(solution)/shard_map/psum | solution.py:9
  62.2 1.1 copy-start.7
  62.2 170.2 %all-gather.19.cloned.1.call-start = ((), (), s32[]{:S(2)}) async-start(), calls=%async_computation.5 | async-start | bytes 3342336 | tf_op jit(solution)/shard_map/all_gather | solution.py:24
  64.2 215.6 %all-gather.21.cloned.1.call-start = ((), (), s32[]{:S(2)}) async-start(), calls=%async_computation.6 | async-start | bytes 1114112 | tf_op jit(solution)/shard_map/all_gather | solution.py:25
  65.0 270.5 %all-gather.23.cloned.1.call-start = ((), (), s32[]{:S(2)}) async-start(), calls=%async_computation.7 | async-start | bytes 3342336 | tf_op jit(solution)/shard_map/all_gather | solution.py:24
  65.6 385.3 %all-reduce.7.cloned.1.call-start = ((), (), s32[]{:S(2)}) async-start(), calls=%async_computation.1 | async-start | bytes 3145728 | tf_op jit(solution)/shard_map/psum | solution.py:9
  177.2 67.1 %copy-start = (f32[512,768]{0,1:T(8,128)S(1)}, f32[512,768]{0,1:T(8,128)}, u32[]{:S(2)}) copy-start(f32[512,768]{0,1:T(8,128)} %all-reduce.5.cloned.1.call-done) | copy-start | bytes 4718596
  281.5 218.0 %all-gather.25.cloned.1.call-start = ((), (), s32[]{:S(2)}) async-start(), calls=%async_computation.8 | async-start | bytes 1114112 | tf_op jit(solution)/shard_map/all_gather | solution.py:25
  282.3 273.0 %all-gather.27.cloned.1.call-start = ((), (), s32[]{:S(2)}) async-start(), calls=%async_computation.9 | async-start | bytes 3342336 | tf_op jit(solution)/shard_map/all_gather | solution.py:24
  283.0 387.8 %all-reduce.9.cloned.1.call-start = ((), (), s32[]{:S(2)}) async-start(), calls=%async_computation.2 | async-start | bytes 3145728 | tf_op jit(solution)/shard_map/psum | solution.py:9
  450.9 12.9 %copy-start.2 = (f32[512,768]{0,1:T(8,128)S(1)}, f32[512,768]{0,1:T(8,128)}, u32[]{:S(2)}) copy-start(f32[512,768]{0,1:T(8,128)} %all-reduce.7.cloned.1.call-done) | copy-start | bytes 4718596
  501.1 218.3 %all-gather.29.cloned.1.call-start = ((), (), s32[]{:S(2)}) async-start(), calls=%async_computation.10 | async-start | bytes 1114112 | tf_op jit(solution)/shard_map/all_gather | solution.py:25
  501.8 273.4 %all-gather.31.cloned.1.call-start = ((), (), s32[]{:S(2)}) async-start(), calls=%async_computation.11 | async-start | bytes 3342336 | tf_op jit(solution)/shard_map/all_gather | solution.py:24
  502.6 388.0 %all-reduce.11.cloned.1.call-start = ((), (), s32[]{:S(2)}) async-start(), calls=%async_computation.3 | async-start | bytes 3145728 | tf_op jit(solution)/shard_map/psum | solution.py:9
  670.9 12.9 %copy-start.1 = (f32[512,768]{0,1:T(8,128)S(1)}, f32[512,768]{0,1:T(8,128)}, u32[]{:S(2)}) copy-start(f32[512,768]{0,1:T(8,128)} %all-reduce.9.cloned.1.call-done) | copy-start | bytes 4718596
  719.4 6.1 copy-start.4
  890.6 13.1 %copy-start.3 = (f32[512,768]{0,1:T(8,128)S(1)}, f32[512,768]{0,1:T(8,128)}, u32[]{:S(2)}) copy-start(f32[512,768]{0,1:T(8,128)} %all-reduce.11.cloned.1.call-done) | copy-start | bytes 4718596
Sparse Core Ops, SparseCore 0:
  9.8 49.4 all-gather.16
  62.3 114.8 all-reduce.4
  179.7 52.6 all-gather.18
  234.6 45.1 all-gather.20
  282.1 53.3 all-gather.22
  337.7 113.1 all-reduce.6
  453.3 46.1 all-gather.24
  501.9 53.3 all-gather.26
  557.7 113.1 all-reduce.8
  673.2 46.1 all-gather.28
  721.8 53.3 all-gather.30
  777.4 113.1 all-reduce.10
where the time goes:
time: 920 us
  waiting for transfers between devices  807 us (88%)
  matrix products  54.9 us (6%)
  local copies, waits for them, and re-layouts  25.7 us (3%)
  other arithmetic  17.1 us (2%)
  between operations  13.7 us (1%)
    psum x4, waiting for transfers between devices, spread(): return lax.psum(jnp.where(mine, x, jnp.zeros_like(x)), axis)  452 us
    all_gather x4, waiting for transfers between devices, per_device(): factor_cols = lax.all_gather(panels_l[k], 'col', axis=1, tiled=True)  204 us
    all_gather x4, waiting for transfers between devices, per_device(): inverse_tile = lax.all_gather(diag_inverse[k], 'col', axis=1, tiled=True)  149 us
    dot_general x4, matrix products, exact_dot(): jnp.dot(left, right, precision=lax.Precision.HIGHEST, preferred_element_t...  50.9 us
  transfers between devices with their start and end apart: 12, of which 12 were waited for; matrix products, arithmetic and copies ran while one was open for 8% of the time, Pallas kernels for 0%

commit v1 on v0

--- a/solution.py
+++ b/solution.py
@@ -22,7 +22,11 @@
     work = rhs
     for k in range(count):
         factor_cols = lax.all_gather(panels_l[k], "col", axis=1, tiled=True)
-        inverse_tile = lax.all_gather(diag_inverse[k], "col", axis=1, tiled=True)
+        part = diag_inverse[k]
+        size = lax.axis_size("col")
+        blocks = jnp.stack([part for _ in range(size)])
+        blocks = lax.all_to_all(blocks, "col", split_axis=0, concat_axis=0)
+        inverse_tile = jnp.concatenate(blocks, axis=1)
         owner = k * width // rows_here
         offset = k * width - owner * rows_here
         strip = work[offset : offset + width]

time: 920 us -> 594 us (0.65)
  waiting for transfers between devices: 807 us -> 454 us
  starting transfers between devices: 0.67 us -> 25.3 us
    all_gather x4, waiting for transfers between devices: 204 us -> 0.08 us  [per_device(): factor_cols = lax.all_gather(panels_l[k], 'col', axis=1, tiled=True)]
    all_gather x4 -> x0, waiting for transfers between devices: 149 us -> none  [per_device(): inverse_tile = lax.all_gather(diag_inverse[k], 'col', axis=1, tiled=True)]
    all_to_all x0 -> x4, starting transfers between devices: none -> 24.7 us  [per_device(): blocks = lax.all_to_all(blocks, 'col', split_axis=0, concat_axis=0)]
    all_to_all x0 -> x4, waiting for transfers between devices: none -> 16 us  [per_device(): blocks = lax.all_to_all(blocks, 'col', split_axis=0, concat_axis=0)]
    psum x4, waiting for transfers between devices: 452 us -> 436 us  [spread(): return lax.psum(jnp.where(mine, x, jnp.zeros_like(x)), axis)]
  transfers between devices with their start and end apart: 12 -> 12, of which waited for: 12 -> 5; matrix products, arithmetic and copies ran while one was open for 8% -> 12% of each run, Pallas kernels for 0% -> 0%
where the time goes in v1:
time: 594 us; the launch traced here: 593 us
  waiting for transfers between devices  454 us (76%)
  matrix products  55.3 us (9%)
  local copies, waits for them, and re-layouts  26 us (4%)
  starting transfers between devices  25.3 us (4%)
  other arithmetic  17 us (3%)
  between operations  15 us (3%)
    psum x4, waiting for transfers between devices, spread(): return lax.psum(jnp.where(mine, x, jnp.zeros_like(x)), axis)  436 us
    dot_general x4, matrix products, exact_dot(): jnp.dot(left, right, precision=lax.Precision.HIGHEST, preferred_element_t...  51.2 us
    all_to_all x4, starting transfers between devices, per_device(): blocks = lax.all_to_all(blocks, 'col', split_axis=0, concat_axis=0)  24.7 us
    all_to_all x4, waiting for transfers between devices, per_device(): blocks = lax.all_to_all(blocks, 'col', split_axis=0, concat_axis=0)  16 us
  transfers between devices with their start and end apart: 12, of which 5 were waited for; matrix products, arithmetic and copies ran while one was open for 12% of the time, Pallas kernels for 0%

profile of v1, /device:TPU:1, one launch (start us, length us, event | category | flops | bytes accessed | tf_op | source)
XLA Modules:
  0.0 593.0 jit_solution(14803463926284162298)
XLA Ops:
  7.4 1.0 slice_bitcast_fusion
  8.3 1.1 stack.12
  9.4 7.6 %all-to-all-start = ((f32[16,512,32]{1,2,0:T(8,128)}), f32[16,512,32]{1,2,0:T(8,128)S(1)}, u32[]{:S(2)}, u32[]{:S(2)}) async-start(f32[16,512,32]{1,2,0:T(8,128)} %stack.12), calls=%async_computation | async-start | bytes 2097152 | tf_op jit(solution)/shard_map/all_to_all | solution.py:28
  17.1 16.0 %all-to-all-done = f32[16,512,32]{1,2,0:T(8,128)S(1)} async-done(((f32[16,512,32]{1,2,0:T(8,128)}), f32[16,512,32]{1,2,0:T(8,128)S(1)}, u32[]{:S(2)}, u32[]{:S(2)}) %all-to-all-start) | async-done | bytes 1048608 | tf_op jit(solution)/shard_map/all_to_all | solution.py:28
  33.0 0.2 conditional.4
  33.0 0.2 broadcast.91.clone
  33.2 1.4 broadcast_select_fusion.3
  34.6 0.0 all-gather.9.cloned.1.call-start
  34.7 1.1 copy-done.4
  35.7 0.9 fusion.20
  36.7 0.0 all-gather.11.cloned.1.call-start
  36.7 0.5 all-gather.11.cloned.1.call-update
  37.3 1.1 stack.13
  38.3 4.2 all-to-all-start.1
  42.6 6.1 %copy.19 = f32[1536,768]{0,1:T(8,128)} copy(f32[1536,768]{1,0:T(8,128)} %param.19) | data formatting | bytes 9437184 | tf_op args[0]
  48.7 102.0 %all-reduce.5.cloned.1.call-done = f32[512,768]{0,1:T(8,128)} async-done(((f32[512,768]{0,1:T(8,128)}), f32[512,768]{0,1:T(8,128)}) %all-reduce.5.cloned.1.call-update) | async-done | bytes 1572880 | tf_op jit(solution)/shard_map/psum | solution.py:9
  150.7 12.1 %subtract_select_fusion.3 = f32[1536,768]{0,1:T(8,128)} fusion(f32[1536,768]{0,1:T(8,128)} %copy.19, f32[512,768]{0,1:T(8,128)} %all-reduce.5.cloned.1.call-done, f32[1,1536,512]{1,2,0:T(8,128)} %all-gather.9.cloned.1.call-done, pred[1536]{0:T(1024)(128)(4,1)S(1)} %fusion.16), kind=kOutput, calls=%fused_computation.11 | convolution fusion | flops 7250116608 | bytes 14157312 | tf_op jit(solution)/shard_map/dot_general | solution.py:13
  162.8 2.9 fusion.15
  165.7 0.4 conditional.5
  165.7 0.2 broadcast.92.clone
  166.0 1.3 broadcast_select_fusion.2
  167.4 0.0 all-gather.13.cloned.1.call-start
  167.4 0.5 all-gather.13.cloned.1.call-update
  167.9 1.1 stack.14
  169.1 6.4 %all-to-all-start.2 = ((f32[16,512,32]{1,2,0:T(8,128)}), f32[16,512,32]{1,2,0:T(8,128)S(1)}, u32[]{:S(2)}, u32[]{:S(2)}) async-start(f32[16,512,32]{1,2,0:T(8,128)} %stack.14), calls=%async_computation.2 | async-start | bytes 2097152 | tf_op jit(solution)/shard_map/all_to_all | solution.py:28
  175.5 0.0 all-reduce.9.cloned.1.call-start
  175.6 112.6 %all-reduce.7.cloned.1.call-done = f32[512,768]{0,1:T(8,128)} async-done(((f32[512,768]{0,1:T(8,128)}), f32[512,768]{0,1:T(8,128)}) %all-reduce.7.cloned.1.call-update) | async-done | bytes 1572880 | tf_op jit(solution)/shard_map/psum | solution.py:9
  288.1 13.0 %subtract_select_fusion.2 = f32[1536,768]{0,1:T(8,128)} fusion(f32[1536,768]{0,1:T(8,128)} %fusion.15, f32[512,768]{0,1:T(8,128)} %all-reduce.7.cloned.1.call-done, f32[1,1536,512]{1,2,0:T(8,128)} %all-gather.11.cloned.1.call-done, pred[1536]{0:T(1024)(128)(4,1)S(1)} %fusion.17), kind=kOutput, calls=%fused_computation.10 | convolution fusion | flops 7250116608 | bytes 14157312 | tf_op jit(solution)/shard_map/dot_general | solution.py:13
  301.1 2.9 fusion.14
  304.0 0.2 conditional.6
  304.0 0.2 broadcast.93.clone
  304.2 1.3 broadcast_select_fusion.1
  305.5 0.0 all-gather.15.cloned.1.call-start
  305.6 0.7 all-gather.15.cloned.1.call-update
  306.3 1.1 stack.15
  307.4 6.5 %all-to-all-start.3 = ((f32[16,512,32]{1,2,0:T(8,128)}), f32[16,512,32]{1,2,0:T(8,128)S(1)}, u32[]{:S(2)}, u32[]{:S(2)}) async-start(f32[16,512,32]{1,2,0:T(8,128)} %stack.15), calls=%async_computation.3 | async-start | bytes 2097152 | tf_op jit(solution)/shard_map/all_to_all | solution.py:28
  313.9 0.3 all-reduce.11.cloned.1.call-start
  314.2 112.1 %all-reduce.9.cloned.1.call-done = f32[512,768]{0,1:T(8,128)} async-done(((f32[512,768]{0,1:T(8,128)}), f32[512,768]{0,1:T(8,128)}) %all-reduce.9.cloned.1.call-update) | async-done | bytes 1572880 | tf_op jit(solution)/shard_map/psum | solution.py:9
  426.4 13.0 %subtract_select_fusion.1 = f32[1536,768]{0,1:T(8,128)} fusion(f32[1536,768]{0,1:T(8,128)} %fusion.14, f32[512,768]{0,1:T(8,128)} %all-reduce.9.cloned.1.call-done, f32[1,1536,512]{1,2,0:T(8,128)} %all-gather.13.cloned.1.call-done, pred[1536]{0:T(1024)(128)(4,1)S(1)} %fusion.18), kind=kOutput, calls=%fused_computation.9 | convolution fusion | flops 7250116608 | bytes 14157312 | tf_op jit(solution)/shard_map/dot_general | solution.py:13
  439.4 2.9 fusion.13
  442.3 10.4 %conditional.7 = (f32[512,768]{0,1:T(8,128)S(1)}) conditional(s32[]{:T(128)} %convert_element_type.9, () %tuple.51, (f32[512,16,32]{0,2,1:T(8,128)S(1)}, f32[1536,768]{0,1:T(8,128)}) %tuple.97), branch_computations={%region_9.10_spmd, %region_10.11_spmd} | conditional | flops 2415919104 | bytes 13631496 | solution.py:34
  442.3 6.1 %copy.25 = f32[1536,768]{1,0:T(8,128)} copy(f32[1536,768]{0,1:T(8,128)} %get-tuple-element.108) | data formatting | bytes 9437184 | tf_op jit(solution)/shard_map
  448.3 4.1 fusion.6
  452.7 1.3 broadcast_select_fusion
  454.1 109.4 %all-reduce.11.cloned.1.call-done = f32[512,768]{0,1:T(8,128)} async-done(((f32[512,768]{0,1:T(8,128)}), f32[512,768]{0,1:T(8,128)}) %all-reduce.11.cloned.1.call-update) | async-done | bytes 1572880 | tf_op jit(solution)/shard_map/psum | solution.py:9
  563.5 13.1 %subtract_select_fusion = f32[1536,768]{0,1:T(8,128)} fusion(f32[1536,768]{0,1:T(8,128)} %fusion.13, f32[512,768]{0,1:T(8,128)} %all-reduce.11.cloned.1.call-done, f32[1,1536,512]{1,2,0:T(8,128)} %all-gather.15.cloned.1.call-done, pred[1536]{0:T(1024)(128)(4,1)S(1)} %fusion.19), kind=kOutput, calls=%fused_computation.8 | convolution fusion | flops 7250116608 | bytes 14157312 | tf_op jit(solution)/shard_map/dot_general | solution.py:13
  576.6 3.0 fusion.12
  579.6 6.0 %copy.27 = f32[1536,768]{1,0:T(8,128)} copy(f32[1536,768]{0,1:T(8,128)} %fusion.12) | data formatting | bytes 9437184 | tf_op jit(solution)/shard_map/scatter | solution.py:43
  (27 shorter events, 0.3 us)
Async XLA Ops:
  9.4 23.6 %all-to-all-start = ((f32[16,512,32]{1,2,0:T(8,128)}), f32[16,512,32]{1,2,0:T(8,128)S(1)}, u32[]{:S(2)}, u32[]{:S(2)}) async-start(f32[16,512,32]{1,2,0:T(8,128)} %stack.12), calls=%async_computation | async-start | bytes 2097152 | tf_op jit(solution)/shard_map/all_to_all | solution.py:28
  17.0 133.7 %all-reduce.5.cloned.1.call-start = ((), (), s32[]{:S(2)}) async-start(), calls=%async_computation.4 | async-start | bytes 3145728 | tf_op jit(solution)/shard_map/psum | solution.py:9
  34.6 1.1 copy-start.4
  34.6 116.0 %all-gather.9.cloned.1.call-start = ((), (), s32[]{:S(2)}) async-start(), calls=%async_computation.8 | async-start | bytes 3342336 | tf_op jit(solution)/shard_map/all_gather | solution.py:24
  36.7 138.9 %all-gather.11.cloned.1.call-start = ((), (), s32[]{:S(2)}) async-start(), calls=%async_computation.9 | async-start | bytes 3342336 | tf_op jit(solution)/shard_map/all_gather | solution.py:24
  38.3 127.3 %all-to-all-start.1 = ((f32[16,512,32]{1,2,0:T(8,128)}), f32[16,512,32]{1,2,0:T(8,128)S(1)}, u32[]{:S(2)}, u32[]{:S(2)}) async-start(f32[16,512,32]{1,2,0:T(8,128)} %stack.13), calls=%async_computation.1 | async-start | bytes 2097152 | tf_op jit(solution)/shard_map/all_to_all | solution.py:28
  42.6 245.6 %all-reduce.7.cloned.1.call-start = ((), (), s32[]{:S(2)}) async-start(), calls=%async_computation.5 | async-start | bytes 3145728 | tf_op jit(solution)/shard_map/psum | solution.py:9
  150.7 12.1 %copy-start = (f32[512,768]{0,1:T(8,128)S(1)}, f32[512,768]{0,1:T(8,128)}, u32[]{:S(2)}) copy-start(f32[512,768]{0,1:T(8,128)} %all-reduce.5.cloned.1.call-done) | copy-start | bytes 4718596
  167.4 146.9 %all-gather.13.cloned.1.call-start = ((), (), s32[]{:S(2)}) async-start(), calls=%async_computation.10 | async-start | bytes 3342336 | tf_op jit(solution)/shard_map/all_gather | solution.py:24
  169.1 134.9 %all-to-all-start.2 = ((f32[16,512,32]{1,2,0:T(8,128)}), f32[16,512,32]{1,2,0:T(8,128)S(1)}, u32[]{:S(2)}, u32[]{:S(2)}) async-start(f32[16,512,32]{1,2,0:T(8,128)} %stack.14), calls=%async_computation.2 | async-start | bytes 2097152 | tf_op jit(solution)/shard_map/all_to_all | solution.py:28
  175.5 250.9 %all-reduce.9.cloned.1.call-start = ((), (), s32[]{:S(2)}) async-start(), calls=%async_computation.6 | async-start | bytes 3145728 | tf_op jit(solution)/shard_map/psum | solution.py:9
  288.1 13.0 %copy-start.2 = (f32[512,768]{0,1:T(8,128)S(1)}, f32[512,768]{0,1:T(8,128)}, u32[]{:S(2)}) copy-start(f32[512,768]{0,1:T(8,128)} %all-reduce.7.cloned.1.call-done) | copy-start | bytes 4718596
  305.5 148.5 %all-gather.15.cloned.1.call-start = ((), (), s32[]{:S(2)}) async-start(), calls=%async_computation.11 | async-start | bytes 3342336 | tf_op jit(solution)/shard_map/all_gather | solution.py:24
  307.4 134.9 %all-to-all-start.3 = ((f32[16,512,32]{1,2,0:T(8,128)}), f32[16,512,32]{1,2,0:T(8,128)S(1)}, u32[]{:S(2)}, u32[]{:S(2)}) async-start(f32[16,512,32]{1,2,0:T(8,128)} %stack.15), calls=%async_computation.3 | async-start | bytes 2097152 | tf_op jit(solution)/shard_map/all_to_all | solution.py:28
  313.9 249.6 %all-reduce.11.cloned.1.call-start = ((), (), s32[]{:S(2)}) async-start(), calls=%async_computation.7 | async-start | bytes 3145728 | tf_op jit(solution)/shard_map/psum | solution.py:9
  426.4 13.0 %copy-start.1 = (f32[512,768]{0,1:T(8,128)S(1)}, f32[512,768]{0,1:T(8,128)}, u32[]{:S(2)}) copy-start(f32[512,768]{0,1:T(8,128)} %all-reduce.9.cloned.1.call-done) | copy-start | bytes 4718596
  563.5 13.1 %copy-start.3 = (f32[512,768]{0,1:T(8,128)S(1)}, f32[512,768]{0,1:T(8,128)}, u32[]{:S(2)}) copy-start(f32[512,768]{0,1:T(8,128)} %all-reduce.11.cloned.1.call-done) | copy-start | bytes 4718596
Sparse Core Ops, SparseCore 0:
  34.7 115.8 all-reduce.4
  167.5 120.5 all-reduce.6
  305.7 120.6 all-reduce.8
  454.1 109.2 all-reduce.10
Sparse Core Ops, SparseCore 1:
  37.5 57.0 all-gather.8
  96.9 51.5 all-gather.10
  170.3 57.9 all-gather.12
  308.8 58.1 all-gather.14
